TPU v7x, 32 devices: a whole 2x2x4 slice. The times are simulated.
32 devices in a mesh: groups: 2 (over y), dp: 8 (over z, x), section: 2 (over core).
Axes of the slice: x: 2, y: 2, z: 4, core: 2. Of those that a mesh axis runs over, the one named last changes fastest.
Arguments:
- boundary: bfloat16 [2, 32, 64, 8192], P('section', ('groups', 'dp')), parts along dimension 1, may hold values from -6 to 6
- w_query: bfloat16 [2, 8192, 128], P('section', 'dp'), may hold values from -8 to 8
- w_key: bfloat16 [2, 8192, 128], P('section', 'dp'), may hold values from -1 to 1
- w_value: bfloat16 [2, 8192, 128], P('section', 'dp'), may hold values from -0.0625 to 0.0625
- w_out: bfloat16 [2, 128, 8192], P('section', None, 'dp'), may hold values from -0.5 to 0.5
- norm_gain: bfloat16 [2, 8192], P('section'), may hold values from 0.099609375 to 1.8984375
- proj_wide: bfloat16 [64, 8192], replicated, may hold values from -0.0625 to 0.0625
- proj_head: bfloat16 [2, 2, 64, 128], P('section'), may hold values from -0.5 to 0.5
- lengths: int32 [32], P(('groups', 'dp')), parts along dimension 0, may hold values from 1 to 64, 614 in all
- owners: int32 [32, 1], P(('groups', 'dp')), parts along dimension 0, may hold values from 0 to 7; in each aligned block of 16 rows (0 to 15, 16 to 31, ...) at most 4 rows name the same one
Outputs:
- store: bfloat16 [64, 2, 2, 64, 64], P(('groups', 'dp'), 'section'), parts along dimension 0
There are 2 independent parts, one for each index of `groups`. A program takes and returns all parts, laid end to end along the dimension named above; an argument that names none is the same for every part. Nothing has to cross between parts.
Inputs may be any that keep to these rules, and one draw needn't show every extreme that they name: `owners`: every owner is named by at most 4 examples, a bound that some block reaches. `lengths`: some sequence has exactly 64 tokens.
All inputs are finite; a program needn't handle non-finite values. No bound on the sum of `lengths` on one device may be relied on, other than what follows from the above.
Results may differ from a plain program's by a relative error of at most 0.013.
Values may be sent and summed in bfloat16 or wider, within the bound.
A program may use at most 128 MiB of HBM per device.

v0:
```python
import jax
import jax.numpy as jnp
from jax import lax
from jax.sharding import PartitionSpec as P

CAP = 4
EPSILON = 1e-05
MASKED = -1e30


def passed_along(array, axis, by):
    size = lax.axis_size(axis)
    pairs = [(i, i + by) for i in range(size) if 0 <= i + by < size]
    return lax.ppermute(array, axis, pairs)


def for_sending(array):

    def short(part):
        return part.astype(jnp.bfloat16) if part.dtype == jnp.float32 else part

    return jax.tree.map(short, array)


def section_forward(hidden, zero_probe, w_query, w_key, w_value, w_out, section_gain, seq_length):
    token_count = hidden.shape[0]
    head_size = w_query.shape[1]
    widened = hidden.astype(jnp.float32)
    inverse_rms = lax.rsqrt(jnp.mean(widened * widened, axis=-1, keepdims=True) + EPSILON)
    normed = (widened * inverse_rms * section_gain.astype(jnp.float32)).astype(jnp.bfloat16)
    queries = jnp.dot(normed, w_query, preferred_element_type=jnp.float32).astype(jnp.bfloat16)
    key_vecs = jnp.dot(normed, w_key, preferred_element_type=jnp.float32).astype(jnp.bfloat16)
    values = (
        jnp.dot(normed, w_value, preferred_element_type=jnp.float32).astype(jnp.bfloat16)
        + zero_probe
    )
    scores = lax.dot_general(
        queries, key_vecs, (((1,), (1,)), ((), ())), preferred_element_type=jnp.float32
    ) * head_size ** (-0.5)
    positions = jnp.arange(token_count)
    allowed = (positions[None, :] <= positions[:, None]) & (positions[None, :] < seq_length)
    scores = jnp.where(allowed, scores, MASKED)
    highest = jnp.max(scores, axis=-1, keepdims=True)
    expd = jnp.exp(scores - highest)
    probs = (expd / jnp.sum(expd, axis=-1, keepdims=True)).astype(jnp.bfloat16)
    mixed = jnp.dot(probs, values, preferred_element_type=jnp.float32).astype(jnp.bfloat16)
    result = (widened + jnp.dot(mixed, w_out, preferred_element_type=jnp.float32)).astype(
        jnp.bfloat16
    )
    return (result, (normed, mixed))


def module_blocks(normed, mixed, value_grad, cotangent, proj_wide, head_proj, valid):
    contract = (((1,), (1,)), ((), ()))
    across = (((0,), (0,)), ((), ()))
    valid_col = valid[:, None]
    wide_in = lax.dot_general(
        normed, proj_wide, contract, preferred_element_type=jnp.float32
    ).astype(jnp.bfloat16)
    head_in = lax.dot_general(
        mixed, head_proj[1], contract, preferred_element_type=jnp.float32
    ).astype(jnp.bfloat16)
    value_side = jnp.where(
        valid_col,
        lax.dot_general(value_grad, head_proj[0], contract, preferred_element_type=jnp.float32),
        0.0,
    ).astype(jnp.bfloat16)
    wide_out = jnp.where(
        valid_col,
        lax.dot_general(cotangent, proj_wide, contract, preferred_element_type=jnp.float32),
        0.0,
    ).astype(jnp.bfloat16)
    block_value = lax.dot_general(value_side, wide_in, across, preferred_element_type=jnp.float32)
    block_output = lax.dot_general(wide_out, head_in, across, preferred_element_type=jnp.float32)
    return jnp.stack([block_value, block_output]).astype(jnp.bfloat16)


def shards(
    boundary, w_query, w_key, w_value, w_out, norm_gain, proj_wide, proj_head, lengths, owners
):
    my_section = lax.axis_index("section")
    section_count = lax.axis_size("section")
    my_owner = lax.axis_index("dp")
    micro_count = boundary.shape[1]
    token_count = boundary.shape[2]
    model_width = boundary.shape[3]
    proj_rank = proj_wide.shape[0]
    query_w, key_w, value_w, out_w = (
        lax.all_gather(w_query[0], "dp", axis=0, tiled=True),
        lax.all_gather(w_key[0], "dp", axis=0, tiled=True),
        lax.all_gather(w_value[0], "dp", axis=0, tiled=True),
        lax.all_gather(w_out[0], "dp", axis=1, tiled=True),
    )
    all_owner = lax.all_gather(owners[:, 0], "dp", axis=0, tiled=True)
    ordinal = jnp.arange(all_owner.shape[0])
    earlier = (all_owner[None, :] == all_owner[:, None]) & (ordinal[None, :] < ordinal[:, None])
    all_slot = jnp.sum(earlier.astype(jnp.int32), axis=1)
    slot_ids = jnp.arange(CAP)[:, None]
    section_gain = norm_gain[0]
    head_proj = proj_head[0]
    boundary_slab = boundary[0]
    positions = jnp.arange(token_count)
    zero_probe = jnp.zeros((token_count, query_w.shape[1]), jnp.bfloat16)
    tick_count = micro_count + section_count - 1

    def make_layer(seq_length):

        def layer(hidden, probe_in):
            return section_forward(
                hidden, probe_in, query_w, key_w, value_w, out_w, section_gain, seq_length
            )

        return layer

    saved = jnp.zeros_like(boundary_slab)
    incoming = jnp.zeros((token_count, model_width), jnp.bfloat16)
    for moment in range(tick_count):
        micro_index = moment - my_section
        is_live = (micro_index >= 0) & (micro_index < micro_count)
        chosen_micro = jnp.clip(micro_index, 0, micro_count - 1)
        own_slab = lax.dynamic_index_in_dim(boundary_slab, chosen_micro, 0, keepdims=False)
        hidden = jnp.where(my_section == 0, own_slab, incoming)
        current = lax.dynamic_index_in_dim(saved, chosen_micro, 0, keepdims=False)
        saved = lax.dynamic_update_index_in_dim(
            saved, jnp.where(is_live, hidden, current), chosen_micro, 0
        )
        if moment + 1 < tick_count:
            seq_length = lax.dynamic_index_in_dim(lengths, chosen_micro, 0, keepdims=False)
            result, extra = make_layer(seq_length)(hidden, zero_probe)
            incoming = passed_along(result, "section", 1)
    blocks = jnp.zeros((micro_count, 2, proj_rank, proj_rank), jnp.bfloat16)
    incoming = jnp.zeros((token_count, model_width), jnp.bfloat16)
    for moment in range(tick_count):
        micro_index = moment - (section_count - 1 - my_section)
        is_live = (micro_index >= 0) & (micro_index < micro_count)
        chosen_micro = jnp.clip(micro_index, 0, micro_count - 1)
        seq_length = lax.dynamic_index_in_dim(lengths, chosen_micro, 0, keepdims=False)
        valid = positions < seq_length
        own_slab = lax.dynamic_index_in_dim(boundary_slab, chosen_micro, 0, keepdims=False)
        masked_own = jnp.where(valid[:, None], own_slab, jnp.zeros_like(own_slab))
        cotangent = jnp.where(my_section == section_count - 1, masked_own, incoming)
        hidden = lax.dynamic_index_in_dim(saved, chosen_micro, 0, keepdims=False)
        result, pullback, extra = jax.vjp(make_layer(seq_length), hidden, zero_probe, has_aux=True)
        hidden_grad, value_grad = pullback(cotangent)
        new_blocks = module_blocks(
            extra[0], extra[1], value_grad, cotangent, proj_wide, head_proj, valid
        )
        if moment + 1 < tick_count:
            incoming = jax.tree.map(
                lambda part, own: part.astype(own.dtype),
                passed_along(for_sending(hidden_grad), "section", -1),
                hidden_grad,
            )
        current = lax.dynamic_index_in_dim(blocks, chosen_micro, 0, keepdims=False)
        blocks = lax.dynamic_update_index_in_dim(
            blocks, jnp.where(is_live, new_blocks, current), chosen_micro, 0
        )
    piece = lax.all_gather(blocks, "dp", axis=0, tiled=True)
    piece_rows = piece.shape[0]
    picked = ((all_owner[None, :] == my_owner) & (all_slot[None, :] == slot_ids)).astype(
        jnp.bfloat16
    )
    running = jnp.dot(picked, piece.reshape(piece_rows, -1), preferred_element_type=jnp.float32)
    return running.astype(jnp.bfloat16).reshape(CAP, 1, 2, proj_rank, proj_rank)


def solution(mesh):
    return jax.shard_map(
        shards,
        mesh=mesh,
        in_specs=(
            P("section", ("groups", "dp"), None, None),
            P("section", "dp", None),
            P("section", "dp", None),
            P("section", "dp", None),
            P("section", None, "dp"),
            P("section", None),
            P(),
            P("section", None, None, None),
            P(("groups", "dp")),
            P(("groups", "dp"), None),
        ),
        out_specs=P(("groups", "dp"), "section", None, None, None),
        check_vma=False,
    )
```

profile of v0, /device:TPU:0, one launch (start us, length us, event | category | flops | bytes accessed | tf_op | source)
XLA Modules:
  0.0 332.0 jit_solution(5913133050592107326)
XLA Ops:
  6.5 0.7 all-gather.10.cloned.1.call-update
  7.3 0.7 all-gather.12.cloned.1.call-update
  8.1 0.7 all-gather.14.cloned.1.call-update
  8.8 0.5 all-gather.16.cloned.1.call-update
  9.3 1.2 dynamic-slice.6
  11.2 0.8 bitcast_dynamic-update-slice_fusion.3
  12.0 13.2 %all-reduce = s32[16]{0:T(128)S(1)} all-reduce(s32[16]{0:T(128)S(1)} %bitcast_dynamic-update-slice_fusion.3), channel_id=2, replica_groups=mesh['groups'=2,'dp'=8,'section'=2] {'dp'}, use_global_device_ids=true, to_apply=%add | all-reduce | flops 16 | bytes 128 | tf_op jit(solution)/shard_map/all_gather | solution.py:94
  25.2 0.8 mul.279
  26.1 1.5 fusion.284
  27.5 1.6 fusion.18
  29.1 0.6 iota_compare_fusion.6
  29.8 0.6 iota_compare_fusion.5
  30.3 0.6 iota_compare_fusion.7
  30.9 0.6 iota_compare_fusion.4
  31.6 0.7 iota_compare_fusion.3
  32.6 1.5 bitcast_dynamic-update-slice_fusion.2
  34.1 27.2 %all-gather.10.cloned.1.call-done = bf16[1,8192,128]{2,1,0:T(8,128)(2,1)} async-done(((bf16[1,1024,128]{2,1,0:T(8,128)(2,1)}), bf16[1,8192,128]{2,1,0:T(8,128)(2,1)}) %all-gather.10.cloned.1.call-update) | async-done | bytes 2097168 | tf_op jit(solution)/shard_map/all_gather | solution.py:89
  61.3 2.5 fusion.84
  63.8 47.3 %all-gather.12.cloned.1.call-done = bf16[1,8192,128]{2,1,0:T(8,128)(2,1)} async-done(((bf16[1,1024,128]{2,1,0:T(8,128)(2,1)}), bf16[1,8192,128]{2,1,0:T(8,128)(2,1)}) %all-gather.12.cloned.1.call-update) | async-done | bytes 2097168 | tf_op jit(solution)/shard_map/all_gather | solution.py:90
  111.1 2.6 fusion.285
  113.7 47.2 %all-gather.14.cloned.1.call-done = bf16[1,8192,128]{2,1,0:T(8,128)(2,1)} async-done(((bf16[1,1024,128]{2,1,0:T(8,128)(2,1)}), bf16[1,8192,128]{2,1,0:T(8,128)(2,1)}) %all-gather.14.cloned.1.call-update) | async-done | bytes 2097168 | tf_op jit(solution)/shard_map/all_gather | solution.py:91
  160.9 2.5 fusion.114
  163.3 47.2 %all-gather.16.cloned.1.call-done = bf16[1,128,8192]{2,1,0:T(8,128)(2,1)} async-done(((bf16[1,128,1024]{2,1,0:T(8,128)(2,1)}), bf16[1,128,8192]{2,1,0:T(8,128)(2,1)}) %all-gather.16.cloned.1.call-update) | async-done | bytes 2097168 | tf_op jit(solution)/shard_map/all_gather | solution.py:92
  210.5 3.6 %fusion = bf16[64,8192]{1,0:T(8,128)(2,1)} fusion(bf16[1,128,8192]{2,1,0:T(8,128)(2,1)} %all-gather.16.cloned.1.call-done, bf16[64,128]{1,0:T(8,128)(2,1)S(1)} %fusion.114, bf16[1,2,64,8192]{3,2,1,0:T(8,128)(2,1)} %param.10, s32[]{:T(128)S(6)} %min.20, pred[]{:T(512)S(6)} %eq.63, f32[64,64]{0,1:T(8,128)S(1)} %get-tuple-element.27, f32[64]{0:T(128)S(1)} %fusion.163, ...), kind=kOutput, calls=%fused_computation.2 | convolution fusion | flops 137383936 | bytes 4227589 | tf_op jit(solution)/shard_map/dot_general | solution.py:47
  214.1 1.5 collective-permute-start
  215.6 1.1 constant_dynamic-slice_fusion.1
  216.8 2.5 fusion.129
  219.8 1.0 copy-done.5
  221.1 0.5 fusion.87
  221.6 2.6 fusion.290
  224.2 2.4 fusion.117
  226.6 3.4 %fusion.1 = bf16[64,8192]{1,0:T(8,128)(2,1)} fusion(bf16[64,8192]{1,0:T(8,128)(2,1)} %copy-done.5, bf16[1,128,8192]{2,1,0:T(8,128)(2,1)} %all-gather.16.cloned.1.call-done, bf16[64,128]{1,0:T(8,128)(2,1)S(1)} %fusion.117, f32[64,64]{0,1:T(8,128)S(1)} %get-tuple-element.29, f32[64]{0:T(128)S(1)} %fusion.164, f32[64]{0:T(128)S(1)} %get-tuple-element.28), kind=kOutput, calls=%fused_computation.3 | convolution fusion | flops 136859648 | bytes 4227584 | tf_op jit(solution)/shard_map/dot_general | solution.py:47
  230.1 1.7 collective-permute-start.1
  231.8 1.8 bitcast_dynamic-update-slice_fusion.1
  235.3 0.5 fusion.90
  237.1 0.7 copy-done.6
  238.8 1.9 fusion.141
  240.6 0.6 fusion.140
  241.5 3.7 %convolution_convert_fusion.3 = bf16[64,8192]{1,0:T(8,128)(2,1)} fusion(bf16[1,8192,128]{2,1,0:T(8,128)(2,1)} %all-gather.10.cloned.1.call-done, bf16[64,128]{1,0:T(8,128)(2,1)S(1)} %fusion.105, f32[64,64]{0,1:T(8,128)S(1)} %get-tuple-element.14, pred[64,64]{0,1:T(32,128)(4,1)S(1)} %get-tuple-element.16, f32[64]{0:T(128)S(1)} %negate_divide_fusion.1, ...), kind=kOutput, calls=%fused_computation.7 | convolution fusion | flops 135823360 | bytes 3182912 | tf_op jit(solution)/shard_map/transpose(jvp())/dot_general | solution.py:31
  245.2 3.6 %convolution_convert_fusion.4 = bf16[64,8192]{1,0:T(8,128)(2,1)} fusion(bf16[1,8192,128]{2,1,0:T(8,128)(2,1)} %all-gather.12.cloned.1.call-done, bf16[64,128]{1,0:T(8,128)(2,1)S(1)} %fusion.90, f32[64,64]{0,1:T(8,128)S(1)} %get-tuple-element.14, pred[64,64]{0,1:T(32,128)(4,1)S(1)} %get-tuple-element.16, f32[64]{0:T(128)S(1)} %negate_divide_fusion.1, ...), kind=kOutput, calls=%fused_computation.8 | convolution fusion | flops 135823360 | bytes 3182912 | tf_op jit(solution)/shard_map/transpose(jvp())/dot_general | solution.py:32
  248.8 3.4 %fusion.24 = (f32[64]{0:T(128)S(1)}, f32[64]{0:T(128)S(1)}, f32[64,8192]{1,0:T(8,128)S(1)}) fusion(bf16[2,64,8192]{2,1,0:T(8,128)(2,1)S(1)} %bitcast_dynamic-update-slice_fusion, s32[]{:T(128)S(6)} %min.19, s32[]{:T(128)S(6)} %min.23, f32[8192]{0:T(1024)S(1)} %bitcast.284, bf16[64,8192]{1,0:T(8,128)(2,1)} %convolution_convert_fusion.3, ...), kind=kOutput, calls=%fused_computation.49 | convolution fusion | flops 139984768 | bytes 8438280 | tf_op jit(solution)/shard_map/transpose(jvp())/dot_general | solution.py:34
  252.2 1.8 fusion.16
  254.0 1.4 collective-permute-start.2
  255.5 0.5 fusion.93
  256.1 0.5 fusion.108
  256.8 0.9 copy-done.7
  258.5 0.6 collective-permute-done.2
  259.1 2.8 fusion.153
  261.8 1.8 fusion.143
  263.6 2.8 fusion.132
  266.9 3.6 %convolution_convert_fusion = bf16[64,8192]{1,0:T(8,128)(2,1)} fusion(bf16[1,8192,128]{2,1,0:T(8,128)(2,1)} %all-gather.10.cloned.1.call-done, bf16[64,128]{1,0:T(8,128)(2,1)S(1)} %fusion.108, f32[64,64]{0,1:T(8,128)S(1)} %get-tuple-element.10, pred[64,64]{0,1:T(32,128)(4,1)S(1)} %get-tuple-element.12, f32[64]{0:T(128)S(1)} %negate_divide_fusion, ...), kind=kOutput, calls=%fused_computation.4 | convolution fusion | flops 135823360 | bytes 3182912 | tf_op jit(solution)/shard_map/transpose(jvp())/dot_general | solution.py:31
  270.5 3.6 %convolution_convert_fusion.1 = bf16[64,8192]{1,0:T(8,128)(2,1)} fusion(bf16[1,8192,128]{2,1,0:T(8,128)(2,1)} %all-gather.12.cloned.1.call-done, bf16[64,128]{1,0:T(8,128)(2,1)S(1)} %fusion.93, f32[64,64]{0,1:T(8,128)S(1)} %get-tuple-element.10, pred[64,64]{0,1:T(32,128)(4,1)S(1)} %get-tuple-element.12, f32[64]{0:T(128)S(1)} %negate_divide_fusion, ...), kind=kOutput, calls=%fused_computation.5 | convolution fusion | flops 135823360 | bytes 3182912 | tf_op jit(solution)/shard_map/transpose(jvp())/dot_general | solution.py:32
  274.1 3.3 fusion.28
  277.4 1.6 fusion.17
  279.0 1.5 collective-permute-start.3
  280.5 0.5 fusion.96
  281.1 0.6 fusion.142
  281.7 2.2 fusion.297
  284.0 2.1 fusion.126
  286.4 3.1 fusion.135
  289.8 0.6 fusion.144
  290.4 2.2 fusion.145
  292.7 31.4 %all_gather.23 = bf16[16,2,64,64]{3,2,1,0:T(8,128)(2,1)S(1)} all-gather(bf16[2,2,64,64]{3,2,1,0:T(8,128)(2,1)S(1)} %fusion.157), channel_id=1, replica_groups=mesh['groups'=2,'dp'=8,'section'=2] {'dp'}, dimensions={0}, use_global_device_ids=true | all-gather | bytes 294912 | tf_op jit(solution)/shard_map/all_gather | solution.py:158
  324.7 0.8 reshape.291
  (83 shorter events, 8.3 us)
Async XLA Ops:
  6.5 232.2 %copy-start = (bf16[64,8192]{1,0:T(8,128)(2,1)S(1)}, bf16[64,8192]{1,0:T(8,128)(2,1)}, u32[]{:S(2)}) copy-start(bf16[64,8192]{1,0:T(8,128)(2,1)} %param.16) | copy-start | bytes 3145732
  6.5 54.8 %all-gather.10.cloned.1.call-start = ((), (), s32[]{:S(2)}) async-start(), calls=%async_computation | async-start | bytes 2359296 | tf_op jit(solution)/shard_map/all_gather | solution.py:89
  7.3 103.8 %all-gather.12.cloned.1.call-start = ((), (), s32[]{:S(2)}) async-start(), calls=%async_computation.1 | async-start | bytes 2359296 | tf_op jit(solution)/shard_map/all_gather | solution.py:90
  8.0 152.9 %all-gather.14.cloned.1.call-start = ((), (), s32[]{:S(2)}) async-start(), calls=%async_computation.2 | async-start | bytes 2359296 | tf_op jit(solution)/shard_map/all_gather | solution.py:91
  8.7 201.8 %all-gather.16.cloned.1.call-start = ((), (), s32[]{:S(2)}) async-start(), calls=%async_computation.3 | async-start | bytes 2359296 | tf_op jit(solution)/shard_map/all_gather | solution.py:92
  214.1 2.6 copy-start.1
  214.1 5.1 %collective-permute-start = (bf16[64,8192]{1,0:T(8,128)(2,1)}, bf16[64,8192]{1,0:T(8,128)(2,1)S(1)}, u32[]{:S(2)}, u32[]{:S(2)}) collective-permute-start(bf16[64,8192]{1,0:T(8,128)(2,1)} %fusion), channel_id=1, source_target_pairs={{0,1},{2,3},{4,5},{6,7},{8,9},{10,11},{12,13},{14,15},{16,17},{18,... | collective-permute-start | bytes 3145736 | tf_op jit(solution)/shard_map/ppermute | solution.py:14
  219.2 1.9 copy-start.10
  219.7 1.0 copy-start.5
  230.1 3.9 %copy-start.2 = (bf16[1,2,64,8192]{3,2,1,0:T(8,128)(2,1)S(1)}, bf16[1,2,64,8192]{3,2,1,0:T(8,128)(2,1)}, u32[]{:S(2)}) copy-start(bf16[1,2,64,8192]{3,2,1,0:T(8,128)(2,1)} %param.10) | copy-start | bytes 6291460
  230.1 3.9 %collective-permute-start.1 = (bf16[64,8192]{1,0:T(8,128)(2,1)}, bf16[64,8192]{1,0:T(8,128)(2,1)S(1)}, u32[]{:S(2)}, u32[]{:S(2)}) collective-permute-start(bf16[64,8192]{1,0:T(8,128)(2,1)} %fusion.1), channel_id=1, source_target_pairs={{0,1},{2,3},{4,5},{6,7},{8,9},{10,11},{12,13},{14,15},{16,17},{18,... | collective-permute-start | bytes 3145736 | tf_op jit(solution)/shard_map/ppermute | solution.py:14
  233.7 1.6 copy-start.11
  234.5 1.7 copy-start.8
  236.2 1.6 copy-start.6
  236.7 1.6 copy-start.14
  248.8 3.4 %copy-start.3 = (bf16[1,2,64,8192]{3,2,1,0:T(8,128)(2,1)S(1)}, bf16[1,2,64,8192]{3,2,1,0:T(8,128)(2,1)}, u32[]{:S(2)}) copy-start(bf16[1,2,64,8192]{3,2,1,0:T(8,128)(2,1)} %param.10) | copy-start | bytes 6291460
  252.2 3.3 copy-start.12
  254.0 2.0 copy-start.9
  254.0 5.0 %collective-permute-start.2 = (bf16[64,8192]{1,0:T(8,128)(2,1)}, bf16[64,8192]{1,0:T(8,128)(2,1)}, u32[]{:S(2)}, u32[]{:S(2)}) collective-permute-start(bf16[64,8192]{1,0:T(8,128)(2,1)} %fusion.16), channel_id=1, source_target_pairs={{1,0},{3,2},{5,4},{7,6},{9,8},{11,10},{13,12},{15,14},{17,16},{19,... | collective-permute-start | bytes 3145736 | tf_op jit(solution)/shard_map/ppermute | solution.py:14
  256.1 1.6 copy-start.7
  274.1 3.3 %copy-start.4 = (bf16[64,8192]{1,0:T(8,128)(2,1)S(1)}, bf16[64,8192]{1,0:T(8,128)(2,1)}, u32[]{:S(2)}) copy-start(bf16[64,8192]{1,0:T(8,128)(2,1)} %fusion.153) | copy-start | bytes 3145732
  277.4 3.1 copy-start.13
  279.0 7.4 %collective-permute-start.3 = (bf16[64,8192]{1,0:T(8,128)(2,1)}, bf16[64,8192]{1,0:T(8,128)(2,1)}, u32[]{:S(2)}, u32[]{:S(2)}) collective-permute-start(bf16[64,8192]{1,0:T(8,128)(2,1)} %fusion.17), channel_id=1, source_target_pairs={{1,0},{3,2},{5,4},{7,6},{9,8},{11,10},{13,12},{15,14},{17,16},{19,... | collective-permute-start | bytes 3145736 | tf_op jit(solution)/shard_map/ppermute | solution.py:14
Sparse Core Ops, SparseCore 0:
  9.5 51.8 all-gather.9
  63.4 47.6 all-gather.11
  113.2 47.6 all-gather.13
  162.9 47.5 all-gather.15
where the time goes:
time: 333 us; the launch traced here: 332 us
  waiting for transfers between devices  172 us (52%)
  matrix products  67.7 us (20%)
  blocking collectives  44.6 us (13%)
  other arithmetic  16.9 us (5%)
  between operations  14.3 us (4%)
  local copies, waits for them, and re-layouts  10 us (3%)
  starting transfers between devices  6.16 us (2%)
    all_gather x1, waiting for transfers between devices, shards(): lax.all_gather(w_key[0], 'dp', axis=0, tiled=True)  47.3 us
    all_gather x1, waiting for transfers between devices, shards(): lax.all_gather(w_out[0], 'dp', axis=1, tiled=True)  47.2 us
    all_gather x1, waiting for transfers between devices, shards(): lax.all_gather(w_value[0], 'dp', axis=0, tiled=True)  47.2 us
    all_gather x1, blocking collectives, shards(): piece = lax.all_gather(blocks, 'dp', axis=0, tiled=True)  31.4 us
    all_gather x1, waiting for transfers between devices, shards(): lax.all_gather(w_query[0], 'dp', axis=0, tiled=True)  27.2 us
    dot_general x5, matrix products, section_forward(): jnp.dot(mixed, w_out, preferred_element_type=jnp.float32)  15.4 us
    dot_general x7, matrix products, section_forward(): jnp.dot(normed, w_value, preferred_element_type=jnp.float32)  14.6 us
    all_gather x1, blocking collectives, shards(): all_owner = lax.all_gather(owners[:, 0], 'dp', axis=0, tiled=True)  13.2 us
  transfers between devices with their start and end apart: 8, of which 6 were waited for; matrix products, arithmetic and copies ran while one was open for 10% of the time, Pallas kernels for 0%

commit v1 on v0

--- a/solution.py
+++ b/solution.py
@@ -6,6 +6,23 @@
 CAP = 4
 EPSILON = 1e-05
 MASKED = -1e30
+
+
+def joined_along(blocks, dim):
+    shape = list(blocks.shape[1:])
+    shape[dim] *= blocks.shape[0]
+    return jnp.moveaxis(blocks, 0, dim).reshape(shape)
+
+
+def gather_around(x, axis, dim):
+    size = lax.axis_size(axis)
+    upward = [(i, (i + 1) % size) for i in range(size)]
+    pieces = [x]
+    while len(pieces) < size:
+        pieces.append(lax.ppermute(pieces[-1], axis, upward))
+    position = lax.axis_index(axis)
+    pieces = jnp.stack(pieces)[(position - jnp.arange(size)) % size]
+    return joined_along(pieces, dim)
 
 
 def passed_along(array, axis, by):
@@ -86,7 +103,7 @@
     model_width = boundary.shape[3]
     proj_rank = proj_wide.shape[0]
     query_w, key_w, value_w, out_w = (
-        lax.all_gather(w_query[0], "dp", axis=0, tiled=True),
+        gather_around(w_query[0], "dp", 0),
         lax.all_gather(w_key[0], "dp", axis=0, tiled=True),
         lax.all_gather(w_value[0], "dp", axis=0, tiled=True),
         lax.all_gather(w_out[0], "dp", axis=1, tiled=True),

time: 333 us -> 309 us (0.928)
  waiting for transfers between devices: 172 us -> 119 us
  local copies, waits for them, and re-layouts: 10 us -> 20.9 us
  starting transfers between devices: 6.16 us -> 16.7 us
  other arithmetic: 16.9 us -> 22.1 us
  matrix products: 67.7 us -> 72.1 us
    ppermute x0 -> x7, waiting for transfers between devices: none -> 50.8 us  [gather_around(): pieces.append(lax.ppermute(pieces[-1], axis, upward))]
    all_gather x1, waiting for transfers between devices: 47.3 us -> 0.01 us  [shards(): lax.all_gather(w_key[0], 'dp', axis=0, tiled=True)]
    all_gather x1, waiting for transfers between devices: 47.2 us -> 17.3 us  [shards(): lax.all_gather(w_value[0], 'dp', axis=0, tiled=True)]
    all_gather x1 -> x0, waiting for transfers between devices: 27.2 us -> none  [shards(): lax.all_gather(w_query[0], 'dp', axis=0, tiled=True)]
    ppermute x0 -> x7, starting transfers between devices: none -> 10.6 us  [gather_around(): pieces.append(lax.ppermute(pieces[-1], axis, upward))]
    unnamed x33 -> x50, local copies, waits for them, and re-layouts: 5.87 us -> 12.2 us
    gather x0 -> x1, local copies, waits for them, and re-layouts: none -> 3.75 us  [gather_around(): pieces = jnp.stack(pieces)[(position - jnp.arange(size)) % size]]
    convert_element_type x2, other arithmetic: 3.39 us -> 7.01 us  [section_forward(): widened = hidden.astype(jnp.float32)]
  transfers between devices with their start and end apart: 8 -> 14, of which waited for: 6 -> 11; matrix products, arithmetic and copies ran while one was open for 10% -> 15% of each run, Pallas kernels for 0% -> 0%
where the time goes in v1:
time: 309 us; the launch traced here: 308 us
  waiting for transfers between devices  119 us (39%)
  matrix products  72.1 us (23%)
  blocking collectives  43.1 us (14%)
  other arithmetic  22.1 us (7%)
  local copies, waits for them, and re-layouts  20.9 us (7%)
  starting transfers between devices  16.7 us (5%)
  between operations  14.3 us (5%)
    ppermute x7, waiting for transfers between devices, gather_around(): pieces.append(lax.ppermute(pieces[-1], axis, upward))  50.8 us
    all_gather x1, waiting for transfers between devices, shards(): lax.all_gather(w_out[0], 'dp', axis=1, tiled=True)  47.4 us
    all_gather x1, blocking collectives, shards(): piece = lax.all_gather(blocks, 'dp', axis=0, tiled=True)  31.4 us
    all_gather x1, waiting for transfers between devices, shards(): lax.all_gather(w_value[0], 'dp', axis=0, tiled=True)  17.3 us
    dot_general x5, matrix products, section_forward(): jnp.dot(mixed, w_out, preferred_element_type=jnp.float32)  15.4 us
    dot_general x7, matrix products, section_forward(): jnp.dot(normed, w_value, preferred_element_type=jnp.float32)  15.3 us
    unnamed x50, local copies, waits for them, and re-layouts  12.2 us
    dot_general x4, matrix products, section_forward(): jnp.dot(normed, w_query, preferred_element_type=jnp.float32)  12.1 us
  transfers between devices with their start and end apart: 14, of which 11 were waited for; matrix products, arithmetic and copies ran while one was open for 15% of the time, Pallas kernels for 0%

profile of v1, /device:TPU:0, one launch (start us, length us, event | category | flops | bytes accessed | tf_op | source)
XLA Modules:
  0.0 308.3 jit_solution(9465124294409455852)
XLA Ops:
  8.1 3.0 collective-permute-start
  11.1 1.5 fusion.297
  12.7 1.2 iota_compare_fusion.6
  13.8 1.4 dynamic-slice.6
  15.8 0.8 bitcast_dynamic-update-slice_fusion.10
  17.1 1.1 iota_compare_fusion.5
  18.8 1.9 collective-permute-done
  21.4 11.7 %all-reduce = s32[16]{0:T(128)S(1)} all-reduce(s32[16]{0:T(128)S(1)} %bitcast_dynamic-update-slice_fusion.10), channel_id=2, replica_groups=mesh['groups'=2,'dp'=8,'section'=2] {'dp'}, use_global_device_ids=true, to_apply=%add | all-reduce | flops 16 | bytes 128 | tf_op jit(solution)/shard_map/all_gather | solution.py:111
  34.1 3.7 %collective-permute-done.1 = bf16[1024,128]{1,0:T(8,128)(2,1)} collective-permute-done((bf16[1024,128]{1,0:T(8,128)(2,1)}, bf16[1024,128]{1,0:T(8,128)(2,1)}, u32[]{:S(2)}, u32[]{:S(2)}) %collective-permute-start.1) | collective-permute-done | bytes 262176 | tf_op jit(solution)/shard_map/ppermute | solution.py:22
  37.8 3.7 %collective-permute-start.2 = (bf16[1024,128]{1,0:T(8,128)(2,1)}, bf16[1024,128]{1,0:T(8,128)(2,1)S(1)}, u32[]{:S(2)}, u32[]{:S(2)}) collective-permute-start(bf16[1024,128]{1,0:T(8,128)(2,1)} %collective-permute-done.1), channel_id=1, source_target_pairs={{0,2},{2,4},{4,6},{6,8},{8,10},{10,12},{12,14},{14,0},{1,3},{3,5},... | collective-permute-start | bytes 786440 | tf_op jit(solution)/shard_map/ppermute | solution.py:22
  41.5 1.2 iota_compare_fusion.3
  42.7 0.8 mul.328
  43.5 1.2 broadcast_compare_fusion.2
  44.7 7.6 %collective-permute-done.2 = bf16[1024,128]{1,0:T(8,128)(2,1)S(1)} collective-permute-done((bf16[1024,128]{1,0:T(8,128)(2,1)}, bf16[1024,128]{1,0:T(8,128)(2,1)S(1)}, u32[]{:S(2)}, u32[]{:S(2)}) %collective-permute-start.2) | collective-permute-done | bytes 262176 | tf_op jit(solution)/shard_map/ppermute | solution.py:22
  52.3 2.4 collective-permute-start.3
  54.7 1.6 fusion.39
  56.3 9.7 %collective-permute-done.3 = bf16[1024,128]{1,0:T(8,128)(2,1)S(1)} collective-permute-done((bf16[1024,128]{1,0:T(8,128)(2,1)S(1)}, bf16[1024,128]{1,0:T(8,128)(2,1)S(1)}, u32[]{:S(2)}, u32[]{:S(2)}) %collective-permute-start.3) | collective-permute-done | bytes 262176 | tf_op jit(solution)/shard_map/ppermute | solution.py:22
  66.0 1.2 collective-permute-start.4
  67.1 1.7 bitcast_dynamic-update-slice_fusion.9
  68.8 1.7 bitcast_dynamic-update-slice_fusion.8
  70.5 6.4 %collective-permute-done.4 = bf16[1024,128]{1,0:T(8,128)(2,1)S(1)} collective-permute-done((bf16[1024,128]{1,0:T(8,128)(2,1)S(1)}, bf16[1024,128]{1,0:T(8,128)(2,1)S(1)}, u32[]{:S(2)}, u32[]{:S(2)}) %collective-permute-start.4) | collective-permute-done | bytes 262176 | tf_op jit(solution)/shard_map/ppermute | solution.py:22
  77.3 0.7 bitcast_dynamic-update-slice_fusion.7
  78.7 8.2 %collective-permute-done.5 = bf16[1024,128]{1,0:T(8,128)(2,1)S(1)} collective-permute-done((bf16[1024,128]{1,0:T(8,128)(2,1)S(1)}, bf16[1024,128]{1,0:T(8,128)(2,1)S(1)}, u32[]{:S(2)}, u32[]{:S(2)}) %collective-permute-start.5) | collective-permute-done | bytes 262176 | tf_op jit(solution)/shard_map/ppermute | solution.py:22
  86.9 0.7 bitcast_dynamic-update-slice_fusion.5
  88.4 13.3 %collective-permute-done.6 = bf16[1024,128]{1,0:T(8,128)(2,1)S(1)} collective-permute-done((bf16[1024,128]{1,0:T(8,128)(2,1)S(1)}, bf16[1024,128]{1,0:T(8,128)(2,1)S(1)}, u32[]{:S(2)}, u32[]{:S(2)}) %collective-permute-start.6) | collective-permute-done | bytes 262176 | tf_op jit(solution)/shard_map/ppermute | solution.py:22
  102.4 3.7 %gather_fusion = bf16[8,1024,128]{2,1,0:T(8,128)(2,1)} fusion(bf16[8,1024,128]{2,1,0:T(8,128)(2,1)} %bitcast_dynamic-update-slice_fusion.3, s32[1024]{0:T(1024)S(1)} %pad_clamp_fusion), kind=kCustom, calls=%fused_computation | custom fusion | bytes 4194336 | tf_op jit(solution)/shard_map/gather | solution.py:24
  106.1 2.5 fusion.92
  108.6 2.6 fusion.298
  111.2 17.3 %all-gather.10.cloned.1.call-done = bf16[1,8192,128]{2,1,0:T(8,128)(2,1)} async-done(((bf16[1,1024,128]{2,1,0:T(8,128)(2,1)}), bf16[1,8192,128]{2,1,0:T(8,128)(2,1)}) %all-gather.10.cloned.1.call-update) | async-done | bytes 2097168 | tf_op jit(solution)/shard_map/all_gather | solution.py:108
  128.6 2.5 fusion.107
  131.0 47.4 %all-gather.12.cloned.1.call-done = bf16[1,128,8192]{2,1,0:T(8,128)(2,1)} async-done(((bf16[1,128,1024]{2,1,0:T(8,128)(2,1)}), bf16[1,128,8192]{2,1,0:T(8,128)(2,1)}) %all-gather.12.cloned.1.call-update) | async-done | bytes 2097168 | tf_op jit(solution)/shard_map/all_gather | solution.py:109
  178.4 3.6 %fusion = bf16[64,8192]{1,0:T(8,128)(2,1)} fusion(bf16[1,128,8192]{2,1,0:T(8,128)(2,1)} %all-gather.12.cloned.1.call-done, bf16[64,128]{1,0:T(8,128)(2,1)S(1)} %fusion.107, f32[64,64]{0,1:T(8,128)S(1)} %get-tuple-element.27, f32[64]{0:T(128)S(1)} %fusion.178, f32[64]{0:T(128)S(1)} %get-tuple-element.26, bf16[1,2,64,8192]{3,2,1,0:T(8,128)(2,1)} %param.10, ...), kind=kOutput, calls=%fused_computation.3 | convolution fusion | flops 137383936 | bytes 4227589 | tf_op jit(solution)/shard_map/dot_general | solution.py:64
  182.0 1.5 collective-permute-start.7
  183.5 1.1 constant_dynamic-slice_fusion.1
  184.6 2.5 fusion.122
  187.6 1.0 copy-done.6
  189.5 2.6 fusion.301
  192.1 2.4 fusion.110
  194.5 3.4 %fusion.1 = bf16[64,8192]{1,0:T(8,128)(2,1)} fusion(bf16[64,8192]{1,0:T(8,128)(2,1)} %copy-done.6, bf16[1,128,8192]{2,1,0:T(8,128)(2,1)} %all-gather.12.cloned.1.call-done, bf16[64,128]{1,0:T(8,128)(2,1)S(1)} %fusion.110, f32[64,64]{0,1:T(8,128)S(1)} %get-tuple-element.29, f32[64]{0:T(128)S(1)} %fusion.179, f32[64]{0:T(128)S(1)} %get-tuple-element.28), kind=kOutput, calls=%fused_computation.4 | convolution fusion | flops 136859648 | bytes 4227584 | tf_op jit(solution)/shard_map/dot_general | solution.py:64
  198.0 1.7 collective-permute-start.8
  199.6 1.8 bitcast_dynamic-update-slice_fusion.1
  205.0 0.7 copy-done.7
  206.6 1.9 fusion.134
  209.4 3.6 %convolution_convert_fusion.4 = bf16[64,8192]{1,0:T(8,128)(2,1)} fusion(bf16[1,8192,128]{2,1,0:T(8,128)(2,1)} %all-gather.8.cloned.1.call-done, bf16[64,128]{1,0:T(8,128)(2,1)S(1)} %convolution_convert_fusion.33, f32[64,64]{0,1:T(8,128)S(1)} %get-tuple-element.14, pred[64,64]{0,1:T(32,128)(4,1)S(1)} %get-tuple-element.16, f32[64]{0:T(128)S(1)} %negate_divide_fusion.1, ...), kind=kOutput, calls=%fused_computation.9 | convolution fusion | flops 135823360 | bytes 3182912 | tf_op jit(solution)/shard_map/transpose(jvp())/dot_general | solution.py:49
  212.9 3.7 %fusion.2 = bf16[64,8192]{1,0:T(8,128)(2,1)} fusion(bf16[64,8192]{1,0:T(8,128)(2,1)} %convolution_convert_fusion.4, bf16[64,128]{1,0:T(8,128)(2,1)S(1)} %convolution_convert_fusion.32, bf16[1,8192,128]{2,1,0:T(8,128)(2,1)} %all-gather.10.cloned.1.call-done), kind=kOutput, calls=%fused_computation.11 | convolution fusion | flops 135266304 | bytes 4210688 | tf_op jit(solution)/shard_map/transpose(jvp())/dot_general | solution.py:51
  216.6 4.6 %fusion.25 = (f32[64]{0:T(128)S(1)}, f32[64]{0:T(128)S(1)}, f32[64,8192]{1,0:T(8,128)}) fusion(bf16[2,64,8192]{2,1,0:T(8,128)(2,1)S(1)} %bitcast_dynamic-update-slice_fusion, s32[]{:T(128)S(6)} %min.19, s32[]{:T(128)S(6)} %min.23, f32[8192]{0:T(1024)S(1)} %bitcast.332, bf16[64,8192]{1,0:T(8,128)(2,1)} %fusion.2, bf16[8192,128]{1,0:T(8,128)(2,1)} %bitcast.317, ...), kind=kOutput, calls=%fused_computation.47 | convolution fusion | flops 141590400 | bytes 7410504 | tf_op jit(solution)/shard_map/transpose(jvp())/dot_general | solution.py:48
  221.3 2.2 convolution_convert_fusion.26
  223.6 3.4 %fusion.47 = bf16[64,8192]{1,0:T(8,128)(2,1)} fusion(f32[64,8192]{1,0:T(8,128)} %get-tuple-element.33, f32[64]{0:T(128)S(1)} %multiply_multiply_fusion.1, f32[64]{0:T(128)S(1)} %fusion.252, bf16[2,64,8192]{2,1,0:T(8,128)(2,1)S(1)} %bitcast_dynamic-update-slice_fusion, s32[]{:T(128)S(6)} %min.19, bf16[1,2,64,8192]{3,2,1,0:T(8,128)(2,1)S(1)} %copy-done.4, ...), kind=kLoop, calls=%fused_computation.69 | loop fusion | flops 5242880 | bytes 5243461 | tf_op jit(solution)/shard_map/transpose(jvp())/convert_element_type | solution.py:45
  227.0 1.4 collective-permute-start.9
  230.1 2.0 collective-permute-done.9
  232.0 2.7 fusion.150
  234.7 1.8 fusion.136
  236.5 2.8 fusion.125
  239.8 3.6 %convolution_convert_fusion.1 = bf16[64,8192]{1,0:T(8,128)(2,1)} fusion(bf16[1,8192,128]{2,1,0:T(8,128)(2,1)} %all-gather.8.cloned.1.call-done, bf16[64,128]{1,0:T(8,128)(2,1)S(1)} %convolution_convert_fusion.26, f32[64,64]{0,1:T(8,128)S(1)} %get-tuple-element.10, pred[64,64]{0,1:T(32,128)(4,1)S(1)} %get-tuple-element.12, f32[64]{0:T(128)S(1)} %negate_divide_fusion, ...), kind=kOutput, calls=%fused_computation.6 | convolution fusion | flops 135823360 | bytes 3182912 | tf_op jit(solution)/shard_map/transpose(jvp())/dot_general | solution.py:49
  243.3 3.7 %fusion.6 = bf16[64,8192]{1,0:T(8,128)(2,1)} fusion(bf16[64,8192]{1,0:T(8,128)(2,1)} %convolution_convert_fusion.1, bf16[64,128]{1,0:T(8,128)(2,1)S(1)} %convolution_convert_fusion.22, bf16[1,8192,128]{2,1,0:T(8,128)(2,1)} %all-gather.10.cloned.1.call-done), kind=kOutput, calls=%fused_computation.15 | convolution fusion | flops 135266304 | bytes 4210688 | tf_op jit(solution)/shard_map/transpose(jvp())/dot_general | solution.py:51
  247.0 4.6 %fusion.31 = (f32[64]{0:T(128)S(1)}, f32[64]{0:T(128)S(1)}, f32[64,8192]{1,0:T(8,128)}) fusion(bf16[2,64,8192]{2,1,0:T(8,128)(2,1)S(1)} %bitcast_dynamic-update-slice_fusion, s32[]{:T(128)S(6)} %min.23, s32[]{:T(128)S(6)} %min.24, f32[8192]{0:T(1024)S(1)} %bitcast.336, bf16[64,8192]{1,0:T(8,128)(2,1)} %fusion.6, bf16[8192,128]{1,0:T(8,128)(2,1)} %bitcast.319, ...), kind=kOutput, calls=%fused_computation.53 | convolution fusion | flops 141590400 | bytes 7410504 | tf_op jit(solution)/shard_map/transpose(jvp())/dot_general | solution.py:48
  251.7 3.6 %fusion.48 = bf16[64,8192]{1,0:T(8,128)(2,1)} fusion(f32[64,8192]{1,0:T(8,128)} %get-tuple-element.37, bf16[64,8192]{1,0:T(8,128)(2,1)} %fusion.150, f32[64]{0:T(128)S(1)} %multiply_multiply_fusion, f32[64]{0:T(128)S(1)} %fusion.253, bf16[2,64,8192]{2,1,0:T(8,128)(2,1)S(1)} %bitcast_dynamic-update-slice_fusion, s32[]{:T(128)S(6)} %min.23), kind=kLoop, calls=%fused_computation.70 | loop fusion | flops 4194304 | bytes 5243396 | tf_op jit(solution)/shard_map/transpose(jvp())/convert_element_type | solution.py:45
  255.3 1.5 collective-permute-start.10
  258.0 2.2 fusion.306
  260.3 2.1 fusion.119
  262.7 3.1 %fusion.128 = bf16[64,128]{1,0:T(8,128)(2,1)S(1)} fusion(bf16[1,128,8192]{2,1,0:T(8,128)(2,1)} %all-gather.12.cloned.1.call-done, bf16[64,8192]{1,0:T(8,128)(2,1)} %collective-permute-done.10, bf16[1,2,64,8192]{3,2,1,0:T(8,128)(2,1)} %param.10, s32[]{:T(128)S(6)} %min.24, pred[64]{0:T(512)(128)(4,1)S(1)} %copy-done.17, pred[]{:T(512)S(6)} %eq.66), kind=kOutput, calls=%fused_computation.137 | convolution fusion | flops 135274496 | bytes 4210757 | tf_op jit(solution)/shard_map/transpose(jvp())/dot_general | solution.py:64
  266.7 2.2 fusion.138
  268.9 31.4 %all_gather.19 = bf16[16,2,64,64]{3,2,1,0:T(8,128)(2,1)S(1)} all-gather(bf16[2,2,64,64]{3,2,1,0:T(8,128)(2,1)S(1)} %fusion.172), channel_id=1, replica_groups=mesh['groups'=2,'dp'=8,'section'=2] {'dp'}, dimensions={0}, use_global_device_ids=true | all-gather | bytes 294912 | tf_op jit(solution)/shard_map/all_gather | solution.py:175
  300.9 0.8 reshape.401
  (115 shorter events, 18.6 us)
Async XLA Ops:
  6.5 200.1 %copy-start = (bf16[64,8192]{1,0:T(8,128)(2,1)S(1)}, bf16[64,8192]{1,0:T(8,128)(2,1)}, u32[]{:S(2)}) copy-start(bf16[64,8192]{1,0:T(8,128)(2,1)} %param.16) | copy-start | bytes 3145732
  6.5 99.6 %all-gather.8.cloned.1.call-start = ((), (), s32[]{:S(2)}) async-start(), calls=%async_computation | async-start | bytes 2359296 | tf_op jit(solution)/shard_map/all_gather | solution.py:107
  7.3 121.3 %all-gather.10.cloned.1.call-start = ((), (), s32[]{:S(2)}) async-start(), calls=%async_computation.1 | async-start | bytes 2359296 | tf_op jit(solution)/shard_map/all_gather | solution.py:108
  8.0 170.4 %all-gather.12.cloned.1.call-start = ((), (), s32[]{:S(2)}) async-start(), calls=%async_computation.2 | async-start | bytes 2359296 | tf_op jit(solution)/shard_map/all_gather | solution.py:109
  8.1 12.7 %collective-permute-start = (bf16[1024,128]{1,0:T(8,128)(2,1)}, bf16[1024,128]{1,0:T(8,128)(2,1)}, u32[]{:S(2)}, u32[]{:S(2)}) collective-permute-start(bf16[1024,128]{1,0:T(8,128)(2,1)} %bitcast.342), channel_id=1, source_target_pairs={{0,2},{2,4},{4,6},{6,8},{8,10},{10,12},{12,14},{14,0},{1,3},{3,5},... | collective-permute-start | bytes 786440 | tf_op jit(solution)/shard_map/ppermute | solution.py:22
  13.8 2.9 copy-start.1
  16.6 16.8 %copy-start.13 = (bf16[1,1024,128]{2,1,0:T(8,128)(2,1)S(1)}, bf16[1,1024,128]{2,1,0:T(8,128)(2,1)}, u32[]{:S(2)}) copy-start(bf16[1,1024,128]{2,1,0:T(8,128)(2,1)} %param.11) | copy-start | bytes 786436
  20.7 17.1 %collective-permute-start.1 = (bf16[1024,128]{1,0:T(8,128)(2,1)}, bf16[1024,128]{1,0:T(8,128)(2,1)}, u32[]{:S(2)}, u32[]{:S(2)}) collective-permute-start(bf16[1024,128]{1,0:T(8,128)(2,1)} %collective-permute-done), channel_id=1, source_target_pairs={{0,2},{2,4},{4,6},{6,8},{8,10},{10,12},{12,14},{14,0},{1,3},{3,5},... | collective-permute-start | bytes 786440 | tf_op jit(solution)/shard_map/ppermute | solution.py:22
  33.2 0.9 copy-start.16
  37.8 14.5 %collective-permute-start.2 = (bf16[1024,128]{1,0:T(8,128)(2,1)}, bf16[1024,128]{1,0:T(8,128)(2,1)S(1)}, u32[]{:S(2)}, u32[]{:S(2)}) collective-permute-start(bf16[1024,128]{1,0:T(8,128)(2,1)} %collective-permute-done.1), channel_id=1, source_target_pairs={{0,2},{2,4},{4,6},{6,8},{8,10},{10,12},{12,14},{14,0},{1,3},{3,5},... | collective-permute-start | bytes 786440 | tf_op jit(solution)/shard_map/ppermute | solution.py:22
  52.3 13.7 %collective-permute-start.3 = (bf16[1024,128]{1,0:T(8,128)(2,1)S(1)}, bf16[1024,128]{1,0:T(8,128)(2,1)S(1)}, u32[]{:S(2)}, u32[]{:S(2)}) collective-permute-start(bf16[1024,128]{1,0:T(8,128)(2,1)S(1)} %collective-permute-done.2), channel_id=1, source_target_pairs={{0,2},{2,4},{4,6},{6,8},{8,10},{10,12},{12,14},{14,0},{1,3},{3,5},... | collective-permute-start | bytes 786440 | tf_op jit(solution)/shard_map/ppermute | solution.py:22
  66.0 11.0 %collective-permute-start.4 = (bf16[1024,128]{1,0:T(8,128)(2,1)S(1)}, bf16[1024,128]{1,0:T(8,128)(2,1)S(1)}, u32[]{:S(2)}, u32[]{:S(2)}) collective-permute-start(bf16[1024,128]{1,0:T(8,128)(2,1)S(1)} %collective-permute-done.3), channel_id=1, source_target_pairs={{0,2},{2,4},{4,6},{6,8},{8,10},{10,12},{12,14},{14,0},{1,3},{3,5},... | collective-permute-start | bytes 786440 | tf_op jit(solution)/shard_map/ppermute | solution.py:22
  77.0 10.0 %collective-permute-start.5 = (bf16[1024,128]{1,0:T(8,128)(2,1)S(1)}, bf16[1024,128]{1,0:T(8,128)(2,1)S(1)}, u32[]{:S(2)}, u32[]{:S(2)}) collective-permute-start(bf16[1024,128]{1,0:T(8,128)(2,1)S(1)} %collective-permute-done.4), channel_id=1, source_target_pairs={{0,2},{2,4},{4,6},{6,8},{8,10},{10,12},{12,14},{14,0},{1,3},{3,5},... | collective-permute-start | bytes 786440 | tf_op jit(solution)/shard_map/ppermute | solution.py:22
  86.9 14.7 %collective-permute-start.6 = (bf16[1024,128]{1,0:T(8,128)(2,1)S(1)}, bf16[1024,128]{1,0:T(8,128)(2,1)S(1)}, u32[]{:S(2)}, u32[]{:S(2)}) collective-permute-start(bf16[1024,128]{1,0:T(8,128)(2,1)S(1)} %collective-permute-done.5), channel_id=1, source_target_pairs={{0,2},{2,4},{4,6},{6,8},{8,10},{10,12},{12,14},{14,0},{1,3},{3,5},... | collective-permute-start | bytes 786440 | tf_op jit(solution)/shard_map/ppermute | solution.py:22
  106.1 2.5 copy-start.19
  182.0 2.6 copy-start.2
  182.0 5.1 %collective-permute-start.7 = (bf16[64,8192]{1,0:T(8,128)(2,1)}, bf16[64,8192]{1,0:T(8,128)(2,1)S(1)}, u32[]{:S(2)}, u32[]{:S(2)}) collective-permute-start(bf16[64,8192]{1,0:T(8,128)(2,1)} %fusion), channel_id=1, source_target_pairs={{0,1},{2,3},{4,5},{6,7},{8,9},{10,11},{12,13},{14,15},{16,17},{18,... | collective-permute-start | bytes 3145736 | tf_op jit(solution)/shard_map/ppermute | solution.py:31
  187.1 1.9 copy-start.9
  187.6 1.0 copy-start.6
  187.6 1.9 copy-start.18
  198.0 3.9 %copy-start.3 = (bf16[1,2,64,8192]{3,2,1,0:T(8,128)(2,1)S(1)}, bf16[1,2,64,8192]{3,2,1,0:T(8,128)(2,1)}, u32[]{:S(2)}) copy-start(bf16[1,2,64,8192]{3,2,1,0:T(8,128)(2,1)} %param.10) | copy-start | bytes 6291460
  198.0 3.9 %collective-permute-start.8 = (bf16[64,8192]{1,0:T(8,128)(2,1)}, bf16[64,8192]{1,0:T(8,128)(2,1)S(1)}, u32[]{:S(2)}, u32[]{:S(2)}) collective-permute-start(bf16[64,8192]{1,0:T(8,128)(2,1)} %fusion.1), channel_id=1, source_target_pairs={{0,1},{2,3},{4,5},{6,7},{8,9},{10,11},{12,13},{14,15},{16,17},{18,... | collective-permute-start | bytes 3145736 | tf_op jit(solution)/shard_map/ppermute | solution.py:31
  201.6 1.6 copy-start.5
  202.4 1.7 copy-start.10
  204.1 1.6 copy-start.7
  204.6 1.6 copy-start.14
  221.3 2.3 copy-start.4
  223.6 4.9 %copy-start.11 = (bf16[1,8192,128]{2,1,0:T(8,128)(2,1)S(1)}, bf16[1,8192,128]{2,1,0:T(8,128)(2,1)}, u32[]{:S(2)}) copy-start(bf16[1,8192,128]{2,1,0:T(8,128)(2,1)} %all-gather.8.cloned.1.call-done) | copy-start | bytes 6291460
  227.0 2.2 copy-start.8
  227.0 5.0 %collective-permute-start.9 = (bf16[64,8192]{1,0:T(8,128)(2,1)}, bf16[64,8192]{1,0:T(8,128)(2,1)}, u32[]{:S(2)}, u32[]{:S(2)}) collective-permute-start(bf16[64,8192]{1,0:T(8,128)(2,1)} %fusion.47), channel_id=1, source_target_pairs={{1,0},{3,2},{5,4},{7,6},{9,8},{11,10},{13,12},{15,14},{17,16},{19,... | collective-permute-start | bytes 3145736 | tf_op jit(solution)/shard_map/ppermute | solution.py:31
  251.7 5.1 %copy-start.12 = (bf16[1,8192,128]{2,1,0:T(8,128)(2,1)S(1)}, bf16[1,8192,128]{2,1,0:T(8,128)(2,1)}, u32[]{:S(2)}) copy-start(bf16[1,8192,128]{2,1,0:T(8,128)(2,1)} %all-gather.8.cloned.1.call-done) | copy-start | bytes 6291460
  255.3 7.4 %collective-permute-start.10 = (bf16[64,8192]{1,0:T(8,128)(2,1)}, bf16[64,8192]{1,0:T(8,128)(2,1)}, u32[]{:S(2)}, u32[]{:S(2)}) collective-permute-start(bf16[64,8192]{1,0:T(8,128)(2,1)} %fusion.48), channel_id=1, source_target_pairs={{1,0},{3,2},{5,4},{7,6},{9,8},{11,10},{13,12},{15,14},{17,16},{19,... | collective-permute-start | bytes 3145736 | tf_op jit(solution)/shard_map/ppermute | solution.py:31
  257.3 0.7 copy-start.17
  266.7 34.0 %copy-start.15 = (pred[16]{0:T(512)(128)(4,1)S(1)}, pred[16]{0:T(512)(128)(4,1)}, u32[]{:S(2)}) copy-start(pred[16]{0:T(512)(128)(4,1)} %broadcast_compare_fusion.2) | copy-start | bytes 52
Sparse Core Ops, SparseCore 0:
  9.5 63.0 all-gather.7
  74.7 53.7 all-gather.9
  130.7 47.5 all-gather.11
